TPU v7x, 32 devices: a whole 2x2x4 slice. The times are simulated.
32 devices in a mesh: tp: 4 (over y, core), fsdp: 8 (over z, x).
Axes of the slice: x: 2, y: 2, z: 4, core: 2. Of those that a mesh axis runs over, the one named last changes fastest.
Arguments:
- momentum: float32 [8192, 28672], P('tp', 'fsdp'), may hold values from -6 to 6
- gradient: bfloat16 [8192, 28672], P('tp', 'fsdp'), may hold values from -6 to 6
- basis: float32 [28672, 512], P('fsdp', 'tp'), may hold values from -1 to 1
Outputs:
- new_momentum: float32 [8192, 28672], P('tp', 'fsdp')
- new_basis: float32 [28672, 512], P('fsdp', 'tp')
- left_factor: float32 [8192, 512], P(('tp', 'fsdp'))
All inputs are finite; a program needn't handle non-finite values.
Results may differ from a plain program's by a relative error of at most 0.0003.
Values sent between devices are 32-bit elements; how exact they have to be, the bound alone decides.
A program may use at most 192 MiB of HBM per device.

v0:
```python
import functools

import jax
import jax.numpy as jnp
from jax import lax
from jax.experimental import pallas as pl
from jax.experimental.pallas import tpu as pltpu
from jax.sharding import PartitionSpec as P

keep_rate = 0.95
tiny = 1e-06
highest = lax.Precision.HIGHEST
MESH = pl.DeviceIdType.MESH
BLOCK = 128
PANEL = 8
CHUNK = 256


def product(a, b, dims, precision=highest):
    return lax.dot_general(a, b, ((dims[:1], dims[1:]), ((), ())), precision=precision, preferred_element_type=jnp.float32)


def eliminate_block(m_ref):
    lanes = lax.broadcasted_iota(jnp.int32, (PANEL, BLOCK), 1)
    subs = lax.broadcasted_iota(jnp.int32, (PANEL, BLOCK), 0)
    rows = lax.broadcasted_iota(jnp.int32, (BLOCK, BLOCK), 0)
    columns = lax.broadcasted_iota(jnp.int32, (BLOCK, BLOCK), 1)
    for start in range(0, BLOCK, PANEL):
        panel = m_ref[start:start + PANEL, :]
        heads = [jnp.broadcast_to(panel[:, start + j:start + j + 1], (PANEL, BLOCK)) for j in range(PANEL)]
        for j in range(PANEL):
            head = heads[j]
            pivot = jnp.broadcast_to(head[j:j + 1, :], (PANEL, BLOCK))
            root = lax.rsqrt(pivot)
            root = root * (1.5 - 0.5 * (pivot * root) * root)
            factor = jnp.where(subs > j, head * root, 0.0)
            row = jnp.broadcast_to(panel[j:j + 1, :], (PANEL, BLOCK)) * root
            row = jnp.where(lanes == start + j, root, row)
            kept = jnp.where((lanes == start + j) & (subs > j), 0.0, panel)
            panel = jnp.where(subs == j, row, kept - factor * row)
            for later in range(j + 1, PANEL):
                scaled = jnp.broadcast_to(heads[later][j:j + 1, :], (PANEL, BLOCK)) * root
                heads[later] = heads[later] - factor * scaled
        m_ref[start:start + PANEL, :] = jnp.where(lanes > start + subs, 0.0, panel)
        stop = start + PANEL
        if stop < BLOCK:
            right = jnp.where(lanes >= stop, panel, 0.0)
            own = jnp.where((lanes > start + subs) & (lanes < stop), 0.0, panel)
            update = product(right, own, (0, 0))
            below = m_ref[stop:, :]
            fresh = (columns[stop:] >= start) & (columns[stop:] < stop)
            m_ref[stop:, :] = jnp.where(fresh, 0.0, below) - update[stop:, :]


def chain_kernel(sizes, own_ref, left_ref, turned_ref, current, inverses, back_ref, sketch, packed, gathered, land0, land1, land2,
                 sum0, sum1, sum2, m_ref, send0, recv0, send1, recv1, send2, recv2, send3, recv3, send4, recv4, send5, recv5,
                 own_sem, z_send, z_recv, x_send, x_recv):
    chips, count = sizes
    n = own_ref.shape[1]
    t, f = lax.axis_index("tp"), lax.axis_index("fsdp")
    y, c = t // 2, t % 2
    z, x = f // 2, f % 2
    lines = count // 2
    stages = [
        (2, c, lambda i: {"tp": 2 * y + i}),
        (chips, y, lambda i: {"tp": 2 * i + c}),
        (count, f, lambda i: {"fsdp": i}),
    ]
    barrier = pltpu.get_barrier_semaphore()
    for members, me, device in stages:
        for step in range(1, members):
            pl.semaphore_signal(barrier, inc=1, device_id=device(lax.rem(me + step, members)), device_id_type=MESH)
    own_copy = pltpu.make_async_copy(own_ref, sketch.at[f], own_sem)
    own_copy.start()
    current[...] = own_ref[...]
    pl.semaphore_wait(barrier, sum(members - 1 for members, _, _ in stages))

    def rows(index, size):
        return pl.ds(pl.multiple_of(index * size, size), size)

    def remote(source, target, send, recv, device):
        return pltpu.make_async_remote_copy(src_ref=source, dst_ref=target, send_sem=send, recv_sem=recv,
                                            device_id=device, device_id_type=MESH)

    def exchange(stage, pick, put, send, recv):
        members, me, device = stage
        copies = []
        for step in range(1, members):
            target = lax.rem(me + step, members)
            copies.append(remote(pick(target), put(step), send.at[step], recv.at[step], device(target)))
        for copy in copies:
            copy.start()
        return copies

    along = [remote(own_ref, sketch.at[f], z_send.at[step], z_recv.at[step], {"fsdp": 2 * lax.rem(z + step, lines) + x})
             for step in range(1, lines)]
    across = [remote(sketch.at[2 * i + x], sketch.at[2 * i + x], x_send.at[i], x_recv.at[i], {"fsdp": 2 * z + 1 - x})
              for i in range(lines)]
    blocks = n // BLOCK

    def turn(r, carry):
        place = 0
        places = {}
        for i in range(blocks):
            strip = product(current[:, i * BLOCK:(i + 1) * BLOCK], current[:, i * BLOCK:], (0, 0))
            for j in range(i, blocks):
                packed[place:place + BLOCK, :] = strip[:, (j - i) * BLOCK:(j - i + 1) * BLOCK]
                places[i, j] = place
                place += BLOCK
        started = []
        source, base, size = packed, 0, place
        downs = ((land0, sum0, send0, recv0), (land1, sum1, send1, recv1), (land2, sum2, send2, recv2))
        for stage, (land, total_ref, send, recv) in zip(stages, downs):
            members, me, _ = stage
            size = size // members
            copies = exchange(stage, lambda i: source.at[rows(i, size)], lambda step: land.at[step], send, recv)
            started += copies
            total = source[rows(me, size), :]
            for step in range(1, members):
                copies[step - 1].wait_recv()
                total = total + land[step]
            total_ref[...] = total
            base = base + me * size
            source = total_ref
        gathered[pl.ds(pl.multiple_of(base, size), size), :] = total
        source = sum2
        for stage, (send, recv) in zip(stages[::-1], ((send3, recv3), (send4, recv4), (send5, recv5))):
            members, me, _ = stage
            spot = gathered.at[pl.ds(pl.multiple_of(base, size), size)]
            copies = exchange(stage, lambda i: source, lambda step: spot, send, recv)
            started += copies
            for copy in copies:
                copy.wait_recv()
            base = base - me * size
            size = size * members
            source = gathered.at[pl.ds(pl.multiple_of(base, size), size)]
        for copy in started:
            copy.wait_send()

        @pl.when(r == 0)
        def _():
            for copy in along:
                copy.start()

        @pl.when(r == 1)
        def _():
            own_copy.wait()
            for copy in along:
                copy.wait_recv()
            for copy in across:
                copy.start()

        x_ref = inverses.at[r]
        for i in range(blocks):
            for j in range(i, blocks):
                x_ref[i * BLOCK:(i + 1) * BLOCK, j * BLOCK:(j + 1) * BLOCK] = gathered[places[i, j]:places[i, j] + BLOCK, :]
        inverse_kernel(x_ref, m_ref)
        current[...] = product(current[...], x_ref[...], (1, 1))
        return carry

    lax.fori_loop(0, 2, turn, 0)
    left_ref[...] = current[...]
    back_ref[...] = product(inverses[1], inverses[0], (1, 0))
    size = own_ref.shape[0]
    for copy in across:
        copy.wait_recv()

    def multiply(i, carry):
        turned_ref[:, rows(i, size)] = product(back_ref[...], sketch[i], (1, 1))
        return carry

    lax.fori_loop(0, count, multiply, 0)
    for copy in along + across:
        copy.wait_send()


def inverse_kernel(x_ref, m_ref):
    n = x_ref.shape[0]
    for start in range(0, n, BLOCK):
        stop = start + BLOCK
        m_ref[...] = x_ref[start:stop, start:stop]
        eliminate_block(m_ref)
        diagonal = m_ref[...]
        x_ref[start:stop, start:stop] = diagonal
        if start > 0:
            x_ref[start:stop, :start] = product(diagonal, x_ref[start:stop, :start], (1, 0))
        if stop < n:
            right = product(diagonal, x_ref[start:stop, stop:], (1, 0))
            if start > 0:
                x_ref[stop:, :start] -= product(right, x_ref[start:stop, :start], (0, 0))
            x_ref[stop:, start:stop] = -product(right, diagonal, (0, 0))
            x_ref[stop:, stop:] -= product(right, right, (0, 0))
            x_ref[start:stop, stop:] = jnp.zeros((BLOCK, n - stop), jnp.float32)


def orthonormal_chain(own, chips, count):
    rows, n = own.shape
    blocks = n // BLOCK
    packed = BLOCK * blocks * (blocks + 1) // 2
    dma = pltpu.SemaphoreType.DMA
    f32 = jnp.float32
    half, part = packed // 2, packed // 2 // chips
    return pl.pallas_call(
        functools.partial(chain_kernel, (chips, count)),
        out_shape=[jax.ShapeDtypeStruct((rows, n), f32), jax.ShapeDtypeStruct((n, rows * count), f32)],
        in_specs=[pl.BlockSpec(memory_space=pltpu.VMEM)],
        out_specs=[pl.BlockSpec(memory_space=pltpu.VMEM)] * 2,
        scratch_shapes=[
            pltpu.VMEM((rows, n), f32),
            pltpu.VMEM((2, n, n), f32),
            pltpu.VMEM((n, n), f32),
            pltpu.VMEM((count, rows, n), f32),
            pltpu.VMEM((packed, BLOCK), f32),
            pltpu.VMEM((packed, BLOCK), f32),
            pltpu.VMEM((2, half, BLOCK), f32),
            pltpu.VMEM((chips, part, BLOCK), f32),
            pltpu.VMEM((count, part // count, BLOCK), f32),
            pltpu.VMEM((half, BLOCK), f32),
            pltpu.VMEM((part, BLOCK), f32),
            pltpu.VMEM((part // count, BLOCK), f32),
            pltpu.VMEM((BLOCK, BLOCK), f32),
        ] + [dma((members,)) for members in (2, 2, chips, chips, count, count, count, count, chips, chips, 2, 2)]
        + [dma] + [dma((count // 2,))] * 4,
        compiler_params=pltpu.CompilerParams(collective_id=2, has_side_effects=True, vmem_limit_bytes=40 * 1024 * 1024),
        cost_estimate=pl.CostEstimate(flops=2 * n * n * n * 40, bytes_accessed=16 * n * n, transcendentals=n),
        name="orthonormal_chain",
    )(own)


def inverse_factor(gram):
    n = gram.shape[0]

    def kernel(g_ref, x_ref, m_ref):
        x_ref[...] = g_ref[...]
        inverse_kernel(x_ref, m_ref)

    return pl.pallas_call(
        kernel,
        out_shape=jax.ShapeDtypeStruct((n, n), jnp.float32),
        in_specs=[pl.BlockSpec(memory_space=pltpu.VMEM)],
        out_specs=pl.BlockSpec(memory_space=pltpu.VMEM),
        scratch_shapes=[pltpu.VMEM((BLOCK, BLOCK), jnp.float32)],
        cost_estimate=pl.CostEstimate(flops=2 * n * n * n * 20, bytes_accessed=8 * n * n, transcendentals=n),
        name="inverse_factor",
    )(gram)


def pieces_of(value):
    high = value.astype(jnp.bfloat16)
    rest = value - high.astype(jnp.float32)
    middle = rest.astype(jnp.bfloat16)
    low = (rest - middle.astype(jnp.float32)).astype(jnp.bfloat16)
    return high, middle, low


def sketch_kernel(m_hbm, g_hbm, b_hbm, out_ref, m_buf, g_buf, land, split, part, land_x, summed, land_z,
                  m_sem, g_sem, own_sem, core_send, core_recv, y_send, y_recv, relay_send, relay_recv,
                  x_send, x_recv, z_send, z_recv):
    t, f = lax.axis_index("tp"), lax.axis_index("fsdp")
    y, c = t // 2, t % 2
    z, x = f // 2, f % 2
    width = b_hbm.shape[1]
    depth = m_hbm.shape[1]
    half = depth // 2
    block = m_hbm.shape[0] // 4
    own = block // 2
    core_peer = {"tp": 2 * y + 1 - c}
    y_peer = {"tp": 2 * (1 - y) + c}
    x_peer = {"fsdp": 2 * z + 1 - x}

    def order(j):
        return 2 * ((z // 2 + (3 - j) // 2) % 2) + (z % 2 + (3 - j) % 2) % 2

    barrier = pltpu.get_barrier_semaphore()
    for peer in [core_peer, y_peer, x_peer] + [{"fsdp": 2 * order(j) + x} for j in range(3)]:
        pl.semaphore_signal(barrier, inc=1, device_id=peer, device_id_type=MESH)

    def fetch(s):
        j = s % 4 * (s // 8) + (s // 2) * (1 - s // 8)
        k = (s % 2) * (1 - s // 8) + (s // 12)
        slot = s % 2
        rows = pl.ds(pl.multiple_of(order(j) * block, block), block)
        columns = pl.ds(pl.multiple_of(k * half, half), half)
        return (pltpu.make_async_copy(m_hbm.at[rows, columns], m_buf.at[slot], m_sem.at[slot]),
                pltpu.make_async_copy(g_hbm.at[rows, columns], g_buf.at[slot], g_sem.at[slot]))

    own_copy = pltpu.make_async_copy(b_hbm, land.at[0], own_sem)
    own_copy.start()
    for copy in fetch(0):
        copy.start()
    pl.semaphore_wait(barrier, 6)

    quarter = depth // 4

    def remote(source, target, send, recv, peer):
        return pltpu.make_async_remote_copy(src_ref=source, dst_ref=target, send_sem=send, recv_sem=recv,
                                            device_id=peer, device_id_type=MESH)

    to_core = [remote(b_hbm.at[pl.ds(k * half, half)], land.at[1, pl.ds(k * half, half)],
                      core_send.at[k], core_recv.at[k], core_peer) for k in range(2)]
    to_y = [remote(b_hbm.at[pl.ds(q * quarter, quarter)], land.at[2, pl.ds(q * quarter, quarter)],
                   y_send.at[q], y_recv.at[q], y_peer) for q in range(4)]
    relay = [remote(land.at[2, pl.ds(q * quarter, quarter)], land.at[3, pl.ds(q * quarter, quarter)],
                    relay_send.at[q], relay_recv.at[q], core_peer) for q in range(4)]
    for copy in to_core + to_y:
        copy.start()

    def cut(slot, column, k):
        columns = pl.ds(pl.multiple_of(column * width, width), width)

        def body(i, carry):
            rows = pl.ds(pl.multiple_of(k * half + i * CHUNK, CHUNK), CHUNK)
            high, middle, low = pieces_of(land[slot, rows, :])
            for place, piece in enumerate((high, middle, low, high, middle, high)):
                split[k, i, place * CHUNK:(place + 1) * CHUNK, columns] = piece
            return carry

        lax.fori_loop(0, half // CHUNK, body, 0)

    part[...] = jnp.zeros_like(part)
    own_copy.wait()
    cut(0, c, 0)
    to_core[0].wait_recv()
    cut(1, 1 - c, 0)

    across = [[remote(part.at[n, j, pl.ds(pl.multiple_of((1 - x) * own, own), own)], land_x.at[n, j],
                      x_send.at[n, j], x_recv.at[n, j], x_peer) for j in range(4)] for n in range(2)]
    along = [[remote(summed.at[n, j], land_z.at[n, j], z_send.at[n, j], z_recv.at[n, j],
                     {"fsdp": 2 * order(j) + x}) for j in range(3)] for n in range(2)]

    def add_x(n, j):
        across[n][j].wait_recv()

        def body(i, carry):
            rows = pl.ds(pl.multiple_of(i * 64, 64), 64)
            mine = pl.ds(pl.multiple_of(x * own + i * 64, 64), 64)
            summed[n, j, rows, :] = part[n, j, mine, :] + land_x[n, j, rows, :]
            return carry

        lax.fori_loop(0, own // 64, body, 0)
        if j < 3:
            along[n][j].start()

    before = {}
    after = {}

    def at(table, s, action):
        table.setdefault(s, []).append(action)

    def second_half():
        cut(0, c, 1)
        to_core[1].wait_recv()
        cut(1, 1 - c, 1)

    def pass_on(q):
        to_y[q].wait_recv()
        relay[q].start()

    def other_chip(k):
        cut(2, c, k)
        relay[2 * k].wait_recv()
        relay[2 * k + 1].wait_recv()
        cut(3, 1 - c, k)

    at(before, 1, second_half)
    at(before, 4, lambda: pass_on(0))
    at(before, 7, lambda: pass_on(1))
    at(before, 8, lambda: other_chip(0))
    at(before, 10, lambda: pass_on(2))
    at(before, 12, lambda: pass_on(3))
    at(before, 12, lambda: other_chip(1))
    for j in range(4):
        at(after, 2 * j + 1, lambda j=j: across[0][j].start())
        at(after, 2 * j + 3, lambda j=j: add_x(0, j))
        at(after, 12 + j, lambda j=j: across[1][j].start())
    at(after, 14, lambda: add_x(1, 0))
    at(after, 15, lambda: add_x(1, 1))

    def step(s, carry):
        for copy in fetch(s):
            copy.wait()

        @pl.when(s < 15)
        def _():
            for copy in fetch(s + 1):
                copy.start()

        for when, actions in before.items():
            @pl.when(s == when)
            def _(actions=actions):
                for action in actions:
                    action()

        slot = s % 2
        j = s % 4 * (s // 8) + (s // 2) * (1 - s // 8)
        k = (s % 2) * (1 - s // 8) + (s // 12)
        n = s // 8

        def body(i, inner):
            columns = pl.ds(pl.multiple_of(i * CHUNK, CHUNK), CHUNK)
            value = m_buf[slot, :, columns] + g_buf[slot, :, columns].astype(jnp.float32)
            high, middle, low = pieces_of(value)
            left = jnp.concatenate([high, high, high, middle, middle, low], axis=1)
            part[n, j] += jnp.dot(left, split[k, i], preferred_element_type=jnp.float32)
            return inner

        lax.fori_loop(0, half // CHUNK, body, 0)
        for when, actions in after.items():
            @pl.when(s == when)
            def _(actions=actions):
                for action in actions:
                    action()
        return carry

    lax.fori_loop(0, 16, step, 0)
    add_x(1, 2)
    add_x(1, 3)
    for n in range(2):
        for j in range(3):
            along[n][j].wait_recv()
        columns = pl.ds(pl.multiple_of((y * (1 - n) + (1 - y) * n) * 2 * width, 2 * width), 2 * width)
        out_ref[:, columns] = summed[n, 3] + land_z[n, 0] + land_z[n, 1] + land_z[n, 2]
    for copy in to_core + to_y + relay + across[0] + across[1] + along[0] + along[1]:
        copy.wait_send()


def sketch_rows(momentum, gradient, basis):
    rows, depth = momentum.shape
    width = basis.shape[1]
    block, half = rows // 4, depth // 2
    own = block // 2
    dma = pltpu.SemaphoreType.DMA
    f32 = jnp.float32
    return pl.pallas_call(
        sketch_kernel,
        out_shape=jax.ShapeDtypeStruct((own, 4 * width), f32),
        in_specs=[pl.BlockSpec(memory_space=pl.ANY)] * 3,
        out_specs=pl.BlockSpec(memory_space=pltpu.VMEM),
        scratch_shapes=[
            pltpu.VMEM((2, block, half), f32),
            pltpu.VMEM((2, block, half), jnp.bfloat16),
            pltpu.VMEM((4, depth, width), f32),
            pltpu.VMEM((2, half // CHUNK, 6 * CHUNK, 2 * width), jnp.bfloat16),
            pltpu.VMEM((2, 4, block, 2 * width), f32),
            pltpu.VMEM((2, 4, own, 2 * width), f32),
            pltpu.VMEM((2, 4, own, 2 * width), f32),
            pltpu.VMEM((2, 3, own, 2 * width), f32),
            dma((2,)), dma((2,)), dma, dma((2,)), dma((2,)), dma((4,)), dma((4,)), dma((4,)), dma((4,)),
            dma((2, 4)), dma((2, 4)), dma((2, 3)), dma((2, 3)),
        ],
        compiler_params=pltpu.CompilerParams(collective_id=1, has_side_effects=True, vmem_limit_bytes=60 * 1024 * 1024),
        cost_estimate=pl.CostEstimate(flops=12 * rows * depth * 4 * width, bytes_accessed=12 * rows * depth, transcendentals=0),
        name="sketch_rows",
    )(momentum, gradient, basis)


def right_kernel(count, m_hbm, g_hbm, left_ref, right_ref, basis_ref, m_buf, g_buf, high_ref, low_ref, part, land_c, summed, land_y,
                 rows_ref, squares, land_s, m_sem, g_sem, core_send, core_recv, y_send, y_recv, keep_send, keep_recv,
                 over_send, over_recv, relay_send, relay_recv, s_send, s_recv):
    t, f = lax.axis_index("tp"), lax.axis_index("fsdp")
    y, c = t // 2, t % 2
    rank, depth = left_ref.shape
    width = rank // 4
    steps = part.shape[0]
    core_peer = {"tp": 2 * y + 1 - c}
    y_peer = {"tp": 2 * (1 - y) + c}
    other = 2 * (1 - y) + c

    barrier = pltpu.get_barrier_semaphore()
    for peer in [core_peer, y_peer] + [{"fsdp": lax.rem(f + step, count)} for step in range(1, count)]:
        pl.semaphore_signal(barrier, inc=1, device_id=peer, device_id_type=MESH)

    def fetch(s):
        columns = pl.ds(pl.multiple_of(s * CHUNK, CHUNK), CHUNK)
        return (pltpu.make_async_copy(m_hbm.at[:, columns], m_buf.at[s % 2], m_sem.at[s % 2]),
                pltpu.make_async_copy(g_hbm.at[:, columns], g_buf.at[s % 2], g_sem.at[s % 2]))

    for copy in fetch(0):
        copy.start()

    def remote(source, target, send, recv, peer):
        return pltpu.make_async_remote_copy(src_ref=source, dst_ref=target, send_sem=send, recv_sem=recv,
                                            device_id=peer, device_id_type=MESH)

    def band(index):
        return pl.ds(pl.multiple_of(index * width, width), width)

    def spot(index, s):
        return right_ref.at[band(index), pl.ds(pl.multiple_of(s * CHUNK, CHUNK), CHUNK)]

    def to_core(s, chip):
        return remote(part.at[s, band(2 * chip + 1 - c)], land_c.at[s, chip], core_send.at[s, chip], core_recv.at[s, chip], core_peer)

    def to_y(s):
        return remote(summed.at[s, 1 - y], land_y.at[s], y_send.at[s], y_recv.at[s], y_peer)

    def keep(s):
        return remote(spot(t, s), spot(t, s), keep_send.at[s], keep_recv.at[s], core_peer)

    def over(s):
        return remote(spot(t, s), spot(t, s), over_send.at[s], over_recv.at[s], y_peer)

    def relay(s):
        return remote(spot(other, s), spot(other, s), relay_send.at[s], relay_recv.at[s], core_peer)

    def split(i, carry):
        columns = pl.ds(pl.multiple_of(i * CHUNK, CHUNK), CHUNK)
        value = left_ref[:, columns]
        high = value.astype(jnp.bfloat16)
        high_ref[i] = high
        low_ref[i] = (value - high.astype(jnp.float32)).astype(jnp.bfloat16)
        return carry

    lax.fori_loop(0, depth // CHUNK, split, 0)
    squares[...] = jnp.zeros_like(squares)
    pl.semaphore_wait(barrier, 1 + count)

    def step(s, carry):
        @pl.when(s < steps)
        def _():
            for copy in fetch(s):
                copy.wait()

            @pl.when(s < steps - 1)
            def _():
                for copy in fetch(s + 1):
                    copy.start()

            part[s] = jnp.zeros((rank, CHUNK), jnp.float32)

            def body(i, inner):
                rows = pl.ds(pl.multiple_of(i * CHUNK, CHUNK), CHUNK)
                value = m_buf[s % 2, rows, :] + g_buf[s % 2, rows, :].astype(jnp.float32)
                high = value.astype(jnp.bfloat16)
                low = (value - high.astype(jnp.float32)).astype(jnp.bfloat16)
                left = jnp.concatenate([high_ref[i], high_ref[i], low_ref[i]], axis=1)
                part[s] += jnp.dot(left, jnp.concatenate([high, low, high], axis=0), preferred_element_type=jnp.float32)
                return inner

            lax.fori_loop(0, depth // CHUNK, body, 0)
            for chip in range(2):
                to_core(s, chip).start()

        @pl.when((s >= 1) & (s < steps + 1))
        def _():
            now = s - 1
            for chip in range(2):
                to_core(now, chip).wait_recv()
                summed[now, chip] = part[now, band(2 * chip + c), :] + land_c[now, chip]
            to_y(now).start()

        @pl.when((s >= 4) & (s < steps + 4))
        def _():
            now = s - 4
            to_y(now).wait_recv()
            mine = summed[now, y] + land_y[now]
            right_ref[band(t), pl.ds(pl.multiple_of(now * CHUNK, CHUNK), CHUNK)] = mine
            over(now).start()
            keep(now).start()
            turned = mine.T
            rows_ref[pl.ds(pl.multiple_of(now * CHUNK, CHUNK), CHUNK), :] = turned
            squares[...] += jnp.sum((turned * turned).reshape(CHUNK // 8, 8, width), axis=0)

        @pl.when(s >= 7)
        def _():
            now = s - 7
            over(now).wait_recv()
            relay(now).start()
        return carry

    lax.fori_loop(0, steps + 4, step, 0)
    spread = [remote(squares, land_s.at[step], s_send.at[step], s_recv.at[step], {"fsdp": lax.rem(f + step, count)})
              for step in range(1, count)]
    for copy in spread:
        copy.start()
    total = squares[...]
    for step in range(1, count):
        spread[step - 1].wait_recv()
        total = total + land_s[step]
    scale = jnp.sqrt(jnp.sum(total, axis=0, keepdims=True) + tiny)

    def divide(i, carry):
        rows = pl.ds(pl.multiple_of(i * CHUNK, CHUNK), CHUNK)
        basis_ref[rows, :] = rows_ref[rows, :] / scale
        return carry

    lax.fori_loop(0, steps, divide, 0)

    def last(s, carry):
        over(s).wait_recv()
        relay(s).start()
        return carry

    lax.fori_loop(steps - 3, steps, last, 0)

    def drain(s, carry):
        for chip in range(2):
            to_core(s, chip).wait_send()
        to_y(s).wait_send()
        over(s).wait_send()
        keep(s).wait()
        relay(s).wait()
        return carry

    lax.fori_loop(0, steps, drain, 0)
    for copy in spread:
        copy.wait_send()


def right_columns(momentum, gradient, left, count):
    rows, depth = momentum.shape
    rank = left.shape[0]
    width = rank // 4
    steps = depth // CHUNK
    dma = pltpu.SemaphoreType.DMA
    f32 = jnp.float32
    return pl.pallas_call(
        functools.partial(right_kernel, count),
        out_shape=[jax.ShapeDtypeStruct((rank, depth), f32), jax.ShapeDtypeStruct((depth, width), f32)],
        in_specs=[pl.BlockSpec(memory_space=pl.ANY)] * 2 + [pl.BlockSpec(memory_space=pltpu.VMEM)],
        out_specs=[pl.BlockSpec(memory_space=pltpu.VMEM)] * 2,
        scratch_shapes=[
            pltpu.VMEM((2, rows, CHUNK), f32),
            pltpu.VMEM((2, rows, CHUNK), jnp.bfloat16),
            pltpu.VMEM((rows // CHUNK, rank, CHUNK), jnp.bfloat16),
            pltpu.VMEM((rows // CHUNK, rank, CHUNK), jnp.bfloat16),
            pltpu.VMEM((steps, rank, CHUNK), f32),
            pltpu.VMEM((steps, 2, width, CHUNK), f32),
            pltpu.VMEM((steps, 2, width, CHUNK), f32),
            pltpu.VMEM((steps, width, CHUNK), f32),
            pltpu.VMEM((depth, width), f32),
            pltpu.VMEM((8, width), f32),
            pltpu.VMEM((count, 8, width), f32),
            dma((2,)), dma((2,)), dma((steps, 2)), dma((steps, 2)), dma((steps,)), dma((steps,)), dma((steps,)), dma((steps,)),
            dma((steps,)), dma((steps,)), dma((steps,)), dma((steps,)), dma((count,)), dma((count,)),
        ],
        compiler_params=pltpu.CompilerParams(collective_id=3, has_side_effects=True, vmem_limit_bytes=60 * 1024 * 1024),
        cost_estimate=pl.CostEstimate(flops=6 * rows * depth * rank, bytes_accessed=6 * rows * depth, transcendentals=0),
        name="right_columns",
    )(momentum, gradient, left)


def sketch_own(momentum, gradient, basis, fitting):
    if fitting:
        return sketch_rows(momentum, gradient, basis)
    tile = momentum + gradient.astype(jnp.float32)
    partial_sketch = product(tile, lax.all_gather(basis, "tp", axis=1, tiled=True), (1, 0))
    return lax.psum_scatter(partial_sketch, "fsdp", scatter_dimension=0, tiled=True)


def orthonormal(own):
    inverse = inverse_factor(lax.psum(product(own, own, (0, 0)), ("fsdp", "tp")))
    return product(own, inverse, (1, 1)), inverse


def on_device(momentum, gradient, basis):
    fitting = lax.axis_size("tp") == 4 and lax.axis_size("fsdp") == 8
    own = sketch_own(momentum, gradient, basis, fitting)
    tile = momentum + gradient.astype(jnp.float32)
    if fitting:
        own_left, left = orthonormal_chain(own, lax.axis_size("tp") // 2, lax.axis_size("fsdp"))
        right, new_basis = right_columns(momentum, gradient, left, lax.axis_size("fsdp"))
        change = product(left, (1.0 - keep_rate) * right, (0, 0), lax.Precision.DEFAULT)
        return (tile - change, new_basis, own_left)
    sketch = lax.all_gather(own, "fsdp", axis=0, tiled=True)
    own_first, inverse = orthonormal(own)
    own_left, second = orthonormal(own_first)
    left = product(sketch, product(second, inverse, (1, 0)), (1, 1))
    partial_right = product(tile, left, (0, 0), lax.Precision.HIGH)
    mine = lax.psum_scatter(partial_right, "tp", scatter_dimension=1, tiled=True)
    squares = lax.psum(jnp.sum(mine * mine, axis=0), "fsdp")
    new_basis = mine / jnp.sqrt(squares + tiny)[None, :]
    full_right = lax.all_gather(mine, "tp", axis=1, tiled=True)
    new_momentum = tile - product(left, (1.0 - keep_rate) * full_right, (1, 1), lax.Precision.DEFAULT)
    return (new_momentum, new_basis, own_left)


def solution(mesh):
    placed = (P("tp", "fsdp"), P("tp", "fsdp"), P("fsdp", "tp"))
    return jax.shard_map(
        on_device,
        mesh=mesh,
        in_specs=placed,
        out_specs=(P("tp", "fsdp"), P("fsdp", "tp"), P(("tp", "fsdp"), None)),
        check_vma=False,
    )
```

profile of v0, /device:TPU:0, one launch (start us, length us, event | category | flops | bytes accessed | tf_op | source)
XLA Modules:
  0.0 379.9 jit_solution(10940366542107840143)
XLA Ops:
  0.6 100.4 %sketch_rows.1.own_ref = f32[256,512]{1,0:T(8,128)} custom-call(f32[2048,3584]{1,0:T(8,128)} %m_hbm.3, bf16[2048,3584]{1,0:T(8,128)(2,1)} %g_hbm.3, f32[3584,128]{1,0:T(8,128)} %b_hbm.1), custom_call_target="tpu_custom_call" | custom-call | flops 45097156608 | bytes 88080384 | tf_op jit(solution)/shard_map/sketch_rows/pallas_call | solution.py:434
  101.1 0.0 copy-start.1
  101.1 1.0 copy-done.1
  102.1 144.6 %orthonormal_chain.1 = (f32[256,512]{1,0:T(8,128)S(1)}, f32[512,2048]{1,0:T(8,128)S(1)}) custom-call(f32[256,512]{1,0:T(8,128)S(1)} %copy-done.1), custom_call_target="tpu_custom_call" | custom-call | flops 10737418240 | bytes 4194304 | tf_op jit(solution)/shard_map/orthonormal_chain/pallas_call | solution.py:203
  246.7 0.0 copy-start
  246.7 2.1 copy-done
  248.8 99.5 %right_columns.1 = (f32[512,3584]{1,0:T(8,128)}, f32[3584,128]{1,0:T(8,128)}) custom-call(f32[2048,3584]{1,0:T(8,128)} %m_hbm.3, bf16[2048,3584]{1,0:T(8,128)(2,1)} %g_hbm.3, f32[512,2048]{1,0:T(8,128)} %copy-done), custom_call_target="tpu_custom_call" | custom-call | flops 22548578304 | bytes 44040192 | tf_op jit(solution)/shard_map/right_columns/pallas_call | solution.py:617
  348.3 0.0 copy-start.2
  348.3 29.6 %add_subtract_fusion = f32[2048,3584]{1,0:T(8,128)} fusion(f32[2048,3584]{1,0:T(8,128)} %m_hbm.3, bf16[2048,3584]{1,0:T(8,128)(2,1)} %g_hbm.3, f32[512,2048]{1,0:T(8,128)} %copy-done, f32[512,3584]{1,0:T(8,128)} %get-tuple-element.8), kind=kOutput, calls=%fused_computation | convolution fusion | flops 7540047872 | bytes 84934656 | tf_op jit(solution)/shard_map/dot_general | solution.py:20
  377.9 0.0 copy-done.2
  377.9 1.2 copy.8
  379.1 0.8 copy.9
Async XLA Ops:
  101.1 1.0 copy-start.1
  246.7 2.1 copy-start
  348.3 29.6 %copy-start.2 = (f32[3584,128]{1,0:T(8,128)S(1)}, f32[3584,128]{1,0:T(8,128)}, u32[]{:S(2)}) copy-start(f32[3584,128]{1,0:T(8,128)} %get-tuple-element.15) | copy-start | bytes 5505028
where the time goes:
time: 380 us
  Pallas kernels  344 us (91%)
  matrix products  29.6 us (8%)
  local copies, waits for them, and re-layouts  5.13 us (1%)
    pallas_call x1, Pallas kernels, orthonormal_chain(): pl.pallas_call(functools.partial(chain_kernel, (chips, count)), out_shape...  145 us
    pallas_call x1, Pallas kernels, sketch_rows(): pl.pallas_call(sketch_kernel, out_shape=jax.ShapeDtypeStruct((own, 4 * wi...  100 us
    pallas_call x1, Pallas kernels, right_columns(): pl.pallas_call(functools.partial(right_kernel, count), out_shape=[jax.Sha...  99.5 us
    dot_general x1, matrix products, product(): lax.dot_general(a, b, ((dims[:1], dims[1:]), ((), ())), precision=precisi...  29.6 us

commit v1 on v0

--- a/solution.py
+++ b/solution.py
@@ -12,7 +12,7 @@
 highest = lax.Precision.HIGHEST
 MESH = pl.DeviceIdType.MESH
 BLOCK = 128
-PANEL = 8
+PANEL = 32
 CHUNK = 256
 
 
@@ -21,31 +21,43 @@
 
 
 def eliminate_block(m_ref):
-    lanes = lax.broadcasted_iota(jnp.int32, (PANEL, BLOCK), 1)
-    subs = lax.broadcasted_iota(jnp.int32, (PANEL, BLOCK), 0)
-    rows = lax.broadcasted_iota(jnp.int32, (BLOCK, BLOCK), 0)
+    lanes = lax.broadcasted_iota(jnp.int32, (8, BLOCK), 1)
+    subs = lax.broadcasted_iota(jnp.int32, (8, BLOCK), 0)
+    panel_lanes = lax.broadcasted_iota(jnp.int32, (PANEL, BLOCK), 1)
+    panel_subs = lax.broadcasted_iota(jnp.int32, (PANEL, BLOCK), 0)
     columns = lax.broadcasted_iota(jnp.int32, (BLOCK, BLOCK), 1)
+    groups = PANEL // 8
+
+    def spread(row):
+        return jnp.broadcast_to(row, (8, BLOCK))
+
     for start in range(0, BLOCK, PANEL):
-        panel = m_ref[start:start + PANEL, :]
-        heads = [jnp.broadcast_to(panel[:, start + j:start + j + 1], (PANEL, BLOCK)) for j in range(PANEL)]
+        panel = [m_ref[start + 8 * g:start + 8 * g + 8, :] for g in range(groups)]
+        heads = {(j, g): spread(panel[g][:, start + j:start + j + 1]) for j in range(PANEL) for g in range(j // 8, groups)}
         for j in range(PANEL):
-            head = heads[j]
-            pivot = jnp.broadcast_to(head[j:j + 1, :], (PANEL, BLOCK))
+            first, place = j // 8, j % 8
+            pivot = spread(heads[j, first][place:place + 1, :])
             root = lax.rsqrt(pivot)
-            root = root * (1.5 - 0.5 * (pivot * root) * root)
-            factor = jnp.where(subs > j, head * root, 0.0)
-            row = jnp.broadcast_to(panel[j:j + 1, :], (PANEL, BLOCK)) * root
-            row = jnp.where(lanes == start + j, root, row)
-            kept = jnp.where((lanes == start + j) & (subs > j), 0.0, panel)
-            panel = jnp.where(subs == j, row, kept - factor * row)
+            root = root * (1.5 - (0.5 * pivot * root) * root)
+            factors = {g: heads[j, g] * root for g in range(first, groups)}
             for later in range(j + 1, PANEL):
-                scaled = jnp.broadcast_to(heads[later][j:j + 1, :], (PANEL, BLOCK)) * root
-                heads[later] = heads[later] - factor * scaled
-        m_ref[start:start + PANEL, :] = jnp.where(lanes > start + subs, 0.0, panel)
+                scaled = spread(factors[later // 8][later % 8:later % 8 + 1, :])
+                for g in range(later // 8, groups):
+                    heads[later, g] = heads[later, g] - factors[g] * scaled
+            row = jnp.where(lanes == start + j, root, spread(panel[first][place:place + 1, :]) * root)
+            for g in range(first, groups):
+                if g == first:
+                    below = subs > place
+                    kept = jnp.where((lanes == start + j) & below, 0.0, panel[g])
+                    panel[g] = jnp.where(subs == place, row, kept - jnp.where(below, factors[g], 0.0) * row)
+                else:
+                    panel[g] = jnp.where(lanes == start + j, 0.0, panel[g]) - factors[g] * row
+        whole = jnp.concatenate(panel, axis=0)
+        m_ref[start:start + PANEL, :] = jnp.where(panel_lanes > start + panel_subs, 0.0, whole)
         stop = start + PANEL
         if stop < BLOCK:
-            right = jnp.where(lanes >= stop, panel, 0.0)
-            own = jnp.where((lanes > start + subs) & (lanes < stop), 0.0, panel)
+            right = jnp.where(panel_lanes >= stop, whole, 0.0)
+            own = jnp.where((panel_lanes > start + panel_subs) & (panel_lanes < stop), 0.0, whole)
             update = product(right, own, (0, 0))
             below = m_ref[stop:, :]
             fresh = (columns[stop:] >= start) & (columns[stop:] < stop)
@@ -94,9 +106,24 @@
 
     along = [remote(own_ref, sketch.at[f], z_send.at[step], z_recv.at[step], {"fsdp": 2 * lax.rem(z + step, lines) + x})
              for step in range(1, lines)]
-    across = [remote(sketch.at[2 * i + x], sketch.at[2 * i + x], x_send.at[i], x_recv.at[i], {"fsdp": 2 * z + 1 - x})
-              for i in range(lines)]
+    first = [remote(own_ref, sketch.at[f], x_send.at[0], x_recv.at[0], {"fsdp": 2 * z + 1 - x})]
+    across = [remote(sketch.at[2 * lax.rem(z + i, lines) + x], sketch.at[2 * lax.rem(z + i, lines) + x], x_send.at[i], x_recv.at[i],
+                     {"fsdp": 2 * z + 1 - x}) for i in range(1, lines)]
     blocks = n // BLOCK
+
+    def ship(r):
+        @pl.when(r == 0)
+        def _():
+            for copy in along + first:
+                copy.start()
+
+        @pl.when(r == 1)
+        def _():
+            own_copy.wait()
+            for copy in along:
+                copy.wait_recv()
+            for copy in across:
+                copy.start()
 
     def turn(r, carry):
         place = 0
@@ -131,24 +158,13 @@
             started += copies
             for copy in copies:
                 copy.wait_recv()
+            if members == count:
+                ship(r)
             base = base - me * size
             size = size * members
             source = gathered.at[pl.ds(pl.multiple_of(base, size), size)]
         for copy in started:
             copy.wait_send()
-
-        @pl.when(r == 0)
-        def _():
-            for copy in along:
-                copy.start()
-
-        @pl.when(r == 1)
-        def _():
-            own_copy.wait()
-            for copy in along:
-                copy.wait_recv()
-            for copy in across:
-                copy.start()
 
         x_ref = inverses.at[r]
         for i in range(blocks):
@@ -162,15 +178,19 @@
     left_ref[...] = current[...]
     back_ref[...] = product(inverses[1], inverses[0], (1, 0))
     size = own_ref.shape[0]
-    for copy in across:
+
+    def multiply(side):
+        def body(i, carry):
+            turned_ref[:, rows(2 * i + side, size)] = product(back_ref[...], sketch[2 * i + side], (1, 1))
+            return carry
+
+        lax.fori_loop(0, lines, body, 0)
+
+    multiply(x)
+    for copy in first + across:
         copy.wait_recv()
-
-    def multiply(i, carry):
-        turned_ref[:, rows(i, size)] = product(back_ref[...], sketch[i], (1, 1))
-        return carry
-
-    lax.fori_loop(0, count, multiply, 0)
-    for copy in along + across:
+    multiply(1 - x)
+    for copy in along + first + across:
         copy.wait_send()
 
 
@@ -404,7 +424,7 @@
             part[n, j] += jnp.dot(left, split[k, i], preferred_element_type=jnp.float32)
             return inner
 
-        lax.fori_loop(0, half // CHUNK, body, 0)
+        lax.fori_loop(0, half // CHUNK, body, 0, unroll=True)
         for when, actions in after.items():
             @pl.when(s == when)
             def _(actions=actions):
@@ -537,7 +557,7 @@
                 part[s] += jnp.dot(left, jnp.concatenate([high, low, high], axis=0), preferred_element_type=jnp.float32)
                 return inner
 
-            lax.fori_loop(0, depth // CHUNK, body, 0)
+            lax.fori_loop(0, depth // CHUNK, body, 0, unroll=True)
             for chip in range(2):
                 to_core(s, chip).start()
 
@@ -656,12 +676,12 @@
 def on_device(momentum, gradient, basis):
     fitting = lax.axis_size("tp") == 4 and lax.axis_size("fsdp") == 8
     own = sketch_own(momentum, gradient, basis, fitting)
-    tile = momentum + gradient.astype(jnp.float32)
     if fitting:
         own_left, left = orthonormal_chain(own, lax.axis_size("tp") // 2, lax.axis_size("fsdp"))
         right, new_basis = right_columns(momentum, gradient, left, lax.axis_size("fsdp"))
         change = product(left, (1.0 - keep_rate) * right, (0, 0), lax.Precision.DEFAULT)
-        return (tile - change, new_basis, own_left)
+        return (momentum + gradient.astype(jnp.float32) - change, new_basis, own_left)
+    tile = momentum + gradient.astype(jnp.float32)
     sketch = lax.all_gather(own, "fsdp", axis=0, tiled=True)
     own_first, inverse = orthonormal(own)
     own_left, second = orthonormal(own_first)

time: 380 us -> 333 us (0.88)
  Pallas kernels: 344 us -> 298 us
    pallas_call x1, Pallas kernels: 145 us -> 114 us  [orthonormal_chain(): pl.pallas_call(functools.partial(chain_kernel, (chips, count)), out_shape...]
    pallas_call x1, Pallas kernels: 100 us -> 87.9 us  [sketch_rows(): pl.pallas_call(sketch_kernel, out_shape=jax.ShapeDtypeStruct((own, 4 * wi...]
where the time goes in v1:
time: 333 us
  Pallas kernels  298 us (89%)
  matrix products  29.6 us (9%)
  local copies, waits for them, and re-layouts  5.13 us (2%)
    pallas_call x1, Pallas kernels, orthonormal_chain(): pl.pallas_call(functools.partial(chain_kernel, (chips, count)), out_shape...  114 us
    pallas_call x1, Pallas kernels, right_columns(): pl.pallas_call(functools.partial(right_kernel, count), out_shape=[jax.Sha...  96.1 us
    pallas_call x1, Pallas kernels, sketch_rows(): pl.pallas_call(sketch_kernel, out_shape=jax.ShapeDtypeStruct((own, 4 * wi...  87.9 us
    dot_general x1, matrix products, product(): lax.dot_general(a, b, ((dims[:1], dims[1:]), ((), ())), precision=precisi...  29.6 us

profile of v1, /device:TPU:0, one launch (start us, length us, event | category | flops | bytes accessed | tf_op | source)
XLA Modules:
  0.0 333.0 jit_solution(606112062145947074)
XLA Ops:
  0.6 87.9 %sketch_rows.1.own_ref = f32[256,512]{1,0:T(8,128)} custom-call(f32[2048,3584]{1,0:T(8,128)} %m_hbm.3, bf16[2048,3584]{1,0:T(8,128)(2,1)} %g_hbm.3, f32[3584,128]{1,0:T(8,128)} %b_hbm.1), custom_call_target="tpu_custom_call" | custom-call | flops 45097156608 | bytes 88080384 | tf_op jit(solution)/shard_map/sketch_rows/pallas_call | solution.py:454
  88.5 0.0 copy-start.1
  88.5 1.0 copy-done.1
  89.6 113.6 %orthonormal_chain.1 = (f32[256,512]{1,0:T(8,128)S(1)}, f32[512,2048]{1,0:T(8,128)S(1)}) custom-call(f32[256,512]{1,0:T(8,128)S(1)} %copy-done.1), custom_call_target="tpu_custom_call" | custom-call | flops 10737418240 | bytes 4194304 | tf_op jit(solution)/shard_map/orthonormal_chain/pallas_call | solution.py:223
  203.2 0.0 copy-start
  203.2 2.1 copy-done
  205.3 96.1 %right_columns.1 = (f32[512,3584]{1,0:T(8,128)}, f32[3584,128]{1,0:T(8,128)}) custom-call(f32[2048,3584]{1,0:T(8,128)} %m_hbm.3, bf16[2048,3584]{1,0:T(8,128)(2,1)} %g_hbm.3, f32[512,2048]{1,0:T(8,128)} %copy-done), custom_call_target="tpu_custom_call" | custom-call | flops 22548578304 | bytes 44040192 | tf_op jit(solution)/shard_map/right_columns/pallas_call | solution.py:637
  301.4 0.0 copy-start.2
  301.4 29.6 %add_subtract_fusion = f32[2048,3584]{1,0:T(8,128)} fusion(f32[2048,3584]{1,0:T(8,128)} %m_hbm.3, bf16[2048,3584]{1,0:T(8,128)(2,1)} %g_hbm.3, f32[512,2048]{1,0:T(8,128)} %copy-done, f32[512,3584]{1,0:T(8,128)} %get-tuple-element.8), kind=kOutput, calls=%fused_computation | convolution fusion | flops 7540047872 | bytes 84934656 | tf_op jit(solution)/shard_map/dot_general | solution.py:20
  331.0 0.0 copy-done.2
  331.0 1.2 copy.8
  332.2 0.8 copy.9
Async XLA Ops:
  88.5 1.0 copy-start.1
  203.2 2.1 copy-start
  301.4 29.6 %copy-start.2 = (f32[3584,128]{1,0:T(8,128)S(1)}, f32[3584,128]{1,0:T(8,128)}, u32[]{:S(2)}) copy-start(f32[3584,128]{1,0:T(8,128)} %get-tuple-element.15) | copy-start | bytes 5505028

commit v2 on v1

--- a/solution.py
+++ b/solution.py
@@ -66,7 +66,7 @@
 
 def chain_kernel(sizes, own_ref, left_ref, turned_ref, current, inverses, back_ref, sketch, packed, gathered, land0, land1, land2,
                  sum0, sum1, sum2, m_ref, send0, recv0, send1, recv1, send2, recv2, send3, recv3, send4, recv4, send5, recv5,
-                 own_sem, z_send, z_recv, x_send, x_recv):
+                 own_sem, z_send, z_recv, x_send, x_recv, late_send, late_recv):
     chips, count = sizes
     n = own_ref.shape[1]
     t, f = lax.axis_index("tp"), lax.axis_index("fsdp")
@@ -104,11 +104,24 @@
             copy.start()
         return copies
 
-    along = [remote(own_ref, sketch.at[f], z_send.at[step], z_recv.at[step], {"fsdp": 2 * lax.rem(z + step, lines) + x})
+    split = n - BLOCK
+    early, late = pl.ds(0, split), pl.ds(split, BLOCK)
+    mate = 2 * z + 1 - x
+
+    def line(step):
+        return {"fsdp": 2 * lax.rem(z + step, lines) + x}
+
+    along = [remote(own_ref.at[:, early], sketch.at[f, :, early], z_send.at[step], z_recv.at[step], line(step))
              for step in range(1, lines)]
-    first = [remote(own_ref, sketch.at[f], x_send.at[0], x_recv.at[0], {"fsdp": 2 * z + 1 - x})]
-    across = [remote(sketch.at[2 * lax.rem(z + i, lines) + x], sketch.at[2 * lax.rem(z + i, lines) + x], x_send.at[i], x_recv.at[i],
-                     {"fsdp": 2 * z + 1 - x}) for i in range(1, lines)]
+    first = [remote(own_ref, sketch.at[f], x_send.at[0], x_recv.at[0], {"fsdp": mate})]
+    across = []
+    for i in range(1, lines):
+        spot = sketch.at[2 * lax.rem(z + i, lines) + x, :, early]
+        across.append(remote(spot, spot, x_send.at[i], x_recv.at[i], {"fsdp": mate}))
+    rest = [remote(own_ref.at[:, late], sketch.at[f, :, late], late_send.at[0, step], late_recv.at[0, step], line(step))
+            for step in range(1, lines)]
+    mates = [remote(sketch.at[mate, :, late], sketch.at[mate, :, late], late_send.at[1, step], late_recv.at[1, step], line(step))
+             for step in range(1, lines)]
     blocks = n // BLOCK
 
     def ship(r):
@@ -120,6 +133,11 @@
         @pl.when(r == 1)
         def _():
             own_copy.wait()
+            for copy in rest:
+                copy.start()
+            first[0].wait_recv()
+            for copy in mates:
+                copy.start()
             for copy in along:
                 copy.wait_recv()
             for copy in across:
@@ -186,11 +204,13 @@
 
         lax.fori_loop(0, lines, body, 0)
 
+    for copy in rest:
+        copy.wait_recv()
     multiply(x)
-    for copy in first + across:
+    for copy in across + mates:
         copy.wait_recv()
     multiply(1 - x)
-    for copy in along + first + across:
+    for copy in along + first + across + rest + mates:
         copy.wait_send()
 
 
@@ -240,7 +260,7 @@
             pltpu.VMEM((part // count, BLOCK), f32),
             pltpu.VMEM((BLOCK, BLOCK), f32),
         ] + [dma((members,)) for members in (2, 2, chips, chips, count, count, count, count, chips, chips, 2, 2)]
-        + [dma] + [dma((count // 2,))] * 4,
+        + [dma] + [dma((count // 2,))] * 4 + [dma((2, count // 2))] * 2,
         compiler_params=pltpu.CompilerParams(collective_id=2, has_side_effects=True, vmem_limit_bytes=40 * 1024 * 1024),
         cost_estimate=pl.CostEstimate(flops=2 * n * n * n * 40, bytes_accessed=16 * n * n, transcendentals=n),
         name="orthonormal_chain",

time: 333 us -> 319 us (0.958)
  Pallas kernels: 298 us -> 284 us
    pallas_call x1, Pallas kernels: 114 us -> 99.3 us  [orthonormal_chain(): pl.pallas_call(functools.partial(chain_kernel, (chips, count)), out_shape...]
where the time goes in v2:
time: 319 us
  Pallas kernels  284 us (89%)
  matrix products  29.6 us (9%)
  local copies, waits for them, and re-layouts  5.13 us (2%)
    pallas_call x1, Pallas kernels, orthonormal_chain(): pl.pallas_call(functools.partial(chain_kernel, (chips, count)), out_shape...  99.3 us
    pallas_call x1, Pallas kernels, right_columns(): pl.pallas_call(functools.partial(right_kernel, count), out_shape=[jax.Sha...  96.6 us
    pallas_call x1, Pallas kernels, sketch_rows(): pl.pallas_call(sketch_kernel, out_shape=jax.ShapeDtypeStruct((own, 4 * wi...  87.9 us
    dot_general x1, matrix products, product(): lax.dot_general(a, b, ((dims[:1], dims[1:]), ((), ())), precision=precisi...  29.6 us

profile of v2, /device:TPU:0, one launch (start us, length us, event | category | flops | bytes accessed | tf_op | source)
XLA Modules:
  0.0 319.2 jit_solution(13213575348252258446)
XLA Ops:
  0.6 87.9 %sketch_rows.1.own_ref = f32[256,512]{1,0:T(8,128)} custom-call(f32[2048,3584]{1,0:T(8,128)} %m_hbm.3, bf16[2048,3584]{1,0:T(8,128)(2,1)} %g_hbm.3, f32[3584,128]{1,0:T(8,128)} %b_hbm.1), custom_call_target="tpu_custom_call" | custom-call | flops 45097156608 | bytes 88080384 | tf_op jit(solution)/shard_map/sketch_rows/pallas_call | solution.py:474
  88.5 0.0 copy-start.1
  88.5 1.0 copy-done.1
  89.6 99.3 %orthonormal_chain.1 = (f32[256,512]{1,0:T(8,128)S(1)}, f32[512,2048]{1,0:T(8,128)S(1)}) custom-call(f32[256,512]{1,0:T(8,128)S(1)} %copy-done.1), custom_call_target="tpu_custom_call" | custom-call | flops 10737418240 | bytes 4194304 | tf_op jit(solution)/shard_map/orthonormal_chain/pallas_call | solution.py:243
  188.9 0.0 copy-start
  188.9 2.1 copy-done
  191.0 96.6 %right_columns.1 = (f32[512,3584]{1,0:T(8,128)}, f32[3584,128]{1,0:T(8,128)}) custom-call(f32[2048,3584]{1,0:T(8,128)} %m_hbm.3, bf16[2048,3584]{1,0:T(8,128)(2,1)} %g_hbm.3, f32[512,2048]{1,0:T(8,128)} %copy-done), custom_call_target="tpu_custom_call" | custom-call | flops 22548578304 | bytes 44040192 | tf_op jit(solution)/shard_map/right_columns/pallas_call | solution.py:657
  287.6 0.0 copy-start.2
  287.6 29.6 %add_subtract_fusion = f32[2048,3584]{1,0:T(8,128)} fusion(f32[2048,3584]{1,0:T(8,128)} %m_hbm.3, bf16[2048,3584]{1,0:T(8,128)(2,1)} %g_hbm.3, f32[512,2048]{1,0:T(8,128)} %copy-done, f32[512,3584]{1,0:T(8,128)} %get-tuple-element.8), kind=kOutput, calls=%fused_computation | convolution fusion | flops 7540047872 | bytes 84934656 | tf_op jit(solution)/shard_map/dot_general | solution.py:20
  317.2 0.0 copy-done.2
  317.2 1.2 copy.8
  318.4 0.8 copy.9
Async XLA Ops:
  88.5 1.0 copy-start.1
  188.9 2.1 copy-start
  287.6 29.6 %copy-start.2 = (f32[3584,128]{1,0:T(8,128)S(1)}, f32[3584,128]{1,0:T(8,128)}, u32[]{:S(2)}) copy-start(f32[3584,128]{1,0:T(8,128)} %get-tuple-element.15) | copy-start | bytes 5505028
